TPU v7x, 512 devices: a whole 4x8x8 slice. The times are simulated.
512 devices in a mesh: graph: 16 (over y, z_lo), gr: 4 (over z_hi), gc: 8 (over x, core).
Axes of the slice: x: 4, y: 8, z: 8 (z_hi: 4, z_lo: 2; z = z_hi * 2 + z_lo), core: 2. Of those that a mesh axis runs over, the one named last changes fastest.
Arguments:
- x_in: bfloat16 [8192, 256], P(('graph', 'gr', 'gc')), parts along dimension 0, may hold values from -64 to 64
- node_type: int32 [8192], P(('graph', 'gr', 'gc')), parts along dimension 0, may hold values from 0 to 7
- node_mask: int32 [8192], P(('graph', 'gr', 'gc')), parts along dimension 0, may hold values 0 or 1
- adj_cat: int32 [8192, 512], P(('graph', 'gc'), 'gr'), parts along dimension 0, may hold values from 0 to 4
- ori_cat: int32 [8192, 512], P(('graph', 'gc'), 'gr'), parts along dimension 0, may hold values from 0 to 7
- type_table: float32 [8, 256], replicated, may hold values from -6 to 6
- adj_table: float32 [5, 32], replicated, may hold values from -6 to 6
- ori_table: float32 [8, 32], replicated, may hold values from -6 to 6
- w_qkv: bfloat16 [256, 768], replicated, may hold values from -1.5 to 1.5
- w_film: bfloat16 [32, 512], replicated, may hold values from -0.75 to 0.75
- w_edge_out: bfloat16 [256, 32], replicated, may hold values from -0.375 to 0.375
- w_node_out: bfloat16 [256, 256], replicated, may hold values from -0.375 to 0.375
- w_node_up: bfloat16 [256, 512], replicated, may hold values from -0.375 to 0.375
- w_node_down: bfloat16 [512, 256], replicated, may hold values from -0.25 to 0.25
- w_edge_up: bfloat16 [32, 128], replicated, may hold values from -1 to 1
- w_edge_down: bfloat16 [128, 32], replicated, may hold values from -0.5 to 0.5
- node_gain1: float32 [256], replicated, may hold values from 0.25 to 1.75
- node_gain2: float32 [256], replicated, may hold values from 0.25 to 1.75
- edge_gain1: float32 [32], replicated, may hold values from 0.25 to 1.75
- edge_gain2: float32 [32], replicated, may hold values from 0.25 to 1.75
Outputs:
- node_out: bfloat16 [8192, 256], P(('graph', 'gr', 'gc')), parts along dimension 0
- edge_out: bfloat16 [32, 8192, 512], P(None, ('graph', 'gc'), 'gr'), parts along dimension 1
There are 16 independent parts, one for each index of `graph`. A program takes and returns all parts, laid end to end along the dimension named above; an argument that names none is the same for every part. Nothing has to cross between parts.
All inputs are finite; a program needn't handle non-finite values. No bound on the sum of `node_mask` on one device may be relied on, other than what follows from the above.
Results may differ from a plain program's by a relative error of at most 0.0075.
The roundings to bfloat16 on the way count: a program that leaves them out, or rounds other values in their place, can miss the bound.
Values may be sent and summed in bfloat16 or wider, within the bound.
A program may use at most 64 MiB of HBM per device.

v0:
```python
import math
import jax
import jax.numpy as jnp
from jax import lax
from jax.sharding import PartitionSpec as P

HEAD_DIM = 32


def combined_all(value, axis, join):
    pieces = jax.tree.map(lambda part: lax.all_gather(part, axis), value)
    head = jax.tree.map(lambda part: part[0], pieces)
    tail = jax.tree.map(lambda part: part[1:], pieces)
    running, _ = lax.scan(lambda running, slab: (join(running, slab), None), head, tail)
    return running


def layer_norm(values, gain, axis):
    center = values - jnp.mean(values, axis=axis, keepdims=True)
    spread = jnp.mean(center * center, axis=axis, keepdims=True)
    return center / jnp.sqrt(spread + 1e-05) * gain


def combine_stats(earlier, later):
    peak = jnp.maximum(earlier[0], later[0])
    first_factor = jnp.exp(earlier[0] - peak)
    second_factor = jnp.exp(later[0] - peak)
    return (
        peak,
        earlier[1] * first_factor + later[1] * second_factor,
        earlier[2] * first_factor + later[2] * second_factor,
    )


def category_sum(codes, lookup):
    levels = jnp.arange(lookup.shape[0], dtype=jnp.int32)
    onehot = (codes[None] == levels[:, None, None]).astype(jnp.float32)
    return jnp.einsum("acr,af->fcr", onehot, lookup, precision=lax.Precision.HIGHEST)


def body(
    x_in,
    node_type,
    node_mask,
    adj_cat,
    ori_cat,
    type_table,
    adj_table,
    ori_table,
    w_qkv,
    w_film,
    w_edge_out,
    w_node_out,
    w_node_up,
    w_node_down,
    w_edge_up,
    w_edge_down,
    node_gain1,
    node_gain2,
    edge_gain1,
    edge_gain2,
):
    width = w_node_out.shape[0]
    owned = x_in.shape[0]
    col_count, row_count = adj_cat.shape
    column_index = lax.axis_index("gc")
    type_levels = jnp.arange(type_table.shape[0], dtype=jnp.int32)
    type_onehot = (node_type[:, None] == type_levels[None, :]).astype(jnp.float32)
    embedded = jnp.dot(type_onehot, type_table, precision=lax.Precision.HIGHEST)
    nodes0 = (x_in.astype(jnp.float32) + embedded).astype(jnp.bfloat16)
    projected = jnp.dot(nodes0, w_qkv, preferred_element_type=jnp.float32).astype(jnp.bfloat16)
    query_own = projected[:, :width]
    key_own = projected[:, width : 2 * width]
    value_own = projected[:, 2 * width :]
    valid_own = node_mask.astype(jnp.bfloat16)
    query_rows, valid_rows = (
        lax.all_gather(query_own, "gc", axis=0, tiled=True),
        lax.all_gather(valid_own, "gc", axis=0, tiled=True),
    )
    key_all, value_all, valid_all = (
        lax.all_gather(key_own, ("gr", "gc"), axis=0, tiled=True),
        lax.all_gather(value_own, ("gr", "gc"), axis=0, tiled=True),
        lax.all_gather(valid_own, ("gr", "gc"), axis=0, tiled=True),
    )
    first_col = column_index * col_count
    key_cols = lax.dynamic_slice_in_dim(key_all, first_col, col_count, 0)
    value_cols = lax.dynamic_slice_in_dim(value_all, first_col, col_count, 0)
    valid_cols = lax.dynamic_slice_in_dim(valid_all, first_col, col_count, 0)
    edges0 = (category_sum(adj_cat, adj_table) + category_sum(ori_cat, ori_table)).astype(
        jnp.bfloat16
    )
    edge_width = edges0.shape[0]
    score_scale = 1.0 / math.sqrt(HEAD_DIM)
    query_t = query_rows.astype(jnp.float32).T
    key_block = min(16, col_count)
    turns = col_count // key_block

    def sweep(turn, state):
        peak, summed, weighted, messages = state
        begin_at = turn * key_block
        edge_part = lax.dynamic_slice_in_dim(edges0, begin_at, key_block, 1)
        film = jnp.einsum("fjr,fk->kjr", edge_part, w_film, preferred_element_type=jnp.float32)
        key_part = lax.dynamic_slice_in_dim(key_cols, begin_at, key_block, 0).astype(jnp.float32).T
        value_part = (
            lax.dynamic_slice_in_dim(value_cols, begin_at, key_block, 0).astype(jnp.float32).T
        )
        valid_part = lax.dynamic_slice_in_dim(valid_cols, begin_at, key_block, 0)
        scores = (
            key_part[:, :, None] * query_t[:, None, :] * score_scale * (film[:width] + 1.0)
            + film[width:]
        )
        message = jnp.einsum(
            "cjr,cf->fjr",
            scores.astype(jnp.bfloat16),
            w_edge_out,
            preferred_element_type=jnp.float32,
        )
        masked = jnp.where(valid_part[None, :, None] > 0, scores, -1000000000.0)
        new_peak = jnp.maximum(peak, jnp.max(masked, axis=1))
        factor = jnp.exp(peak - new_peak)
        expo = jnp.exp(masked - new_peak[:, None, :])
        summed = summed * factor + jnp.sum(expo, axis=1)
        weighted = weighted * factor + jnp.sum(expo * value_part[:, :, None], axis=1)
        messages = lax.dynamic_update_slice_in_dim(messages, message, begin_at, 1)
        return (new_peak, summed, weighted, messages)

    initial = (
        jnp.full((width, row_count), -1e30, jnp.float32),
        jnp.zeros((width, row_count), jnp.float32),
        jnp.zeros((width, row_count), jnp.float32),
        jnp.zeros((edge_width, col_count, row_count), jnp.float32),
    )
    peak, summed, weighted, messages = lax.fori_loop(0, turns, sweep, initial)
    peak, summed, weighted = combined_all((peak, summed, weighted), "gc", combine_stats)
    attended = lax.dynamic_slice_in_dim(weighted / summed, column_index * owned, owned, 1).T
    valid_node = valid_own.astype(jnp.float32)
    attn_bf = attended.astype(jnp.bfloat16)
    nodes1 = layer_norm(
        nodes0.astype(jnp.float32)
        + jnp.dot(attn_bf, w_node_out, preferred_element_type=jnp.float32),
        node_gain1,
        -1,
    ).astype(jnp.bfloat16)
    hidden_node = jnp.maximum(
        jnp.dot(nodes1, w_node_up, preferred_element_type=jnp.float32), 0.0
    ).astype(jnp.bfloat16)
    node_out = (
        layer_norm(
            nodes1.astype(jnp.float32)
            + jnp.dot(hidden_node, w_node_down, preferred_element_type=jnp.float32),
            node_gain2,
            -1,
        )
        * valid_node[:, None]
    ).astype(jnp.bfloat16)
    edges1 = layer_norm(edges0.astype(jnp.float32) + messages, edge_gain1[:, None, None], 0).astype(
        jnp.bfloat16
    )
    hidden_edge = jnp.maximum(
        jnp.einsum("fjr,fh->hjr", edges1, w_edge_up, preferred_element_type=jnp.float32), 0.0
    ).astype(jnp.bfloat16)
    edges2 = layer_norm(
        edges1.astype(jnp.float32)
        + jnp.einsum("hjr,hf->fjr", hidden_edge, w_edge_down, preferred_element_type=jnp.float32),
        edge_gain2[:, None, None],
        0,
    )
    edge_out = (
        edges2
        * valid_cols.astype(jnp.float32)[None, :, None]
        * valid_rows.astype(jnp.float32)[None, None, :]
    ).astype(jnp.bfloat16)
    return (node_out, edge_out)


def solution(mesh):
    return jax.shard_map(
        body,
        mesh=mesh,
        in_specs=(
            P(("graph", "gr", "gc"), None),
            P(("graph", "gr", "gc")),
            P(("graph", "gr", "gc")),
            P(("graph", "gc"), "gr"),
            P(("graph", "gc"), "gr"),
            P(),
            P(),
            P(),
            P(),
            P(),
            P(),
            P(),
            P(),
            P(),
            P(),
            P(),
            P(),
            P(),
            P(),
            P(),
        ),
        out_specs=(P(("graph", "gr", "gc"), None), P(None, ("graph", "gc"), "gr")),
        check_vma=False,
    )
```

profile of v0, /device:TPU:1, one launch (start us, length us, event | category | flops | bytes accessed | tf_op | source)
XLA Modules:
  0.0 318.0 jit_solution(9639753481749543636)
XLA Ops:
  7.3 1.2 convert_convert_fusion
  8.5 1.3 dynamic-slice
  10.7 76.1 %all-reduce = bf16[512]{0:T(512)(128)(2,1)S(1)} all-reduce(bf16[512]{0:T(512)(128)(2,1)S(1)} %dynamic-update-slice), channel_id=1, replica_groups=mesh['graph'=16,'gr'=4,'gc'=8] {'gr','gc'}, use_global_device_ids=true, to_apply=%add | all-reduce | flops 512 | bytes 2048
  86.8 0.9 fusion.24
  88.3 45.3 %all_gather.36 = bf16[512,256]{1,0:T(8,128)(2,1)S(1)} all-gather(bf16[16,256]{1,0:T(8,128)(2,1)S(1)} %get-tuple-element.348), channel_id=1, replica_groups=mesh['graph'=16,'gr'=4,'gc'=8] {'gr','gc'}, dimensions={0}, use_global_device_ids=true | all-gather | bytes 270336 | tf_op jit(solution)/shard_map/all_gather | solution.py:82
  134.9 41.5 %all_gather.34 = bf16[512,256]{1,0:T(8,128)(2,1)S(1)} all-gather(bf16[16,256]{1,0:T(8,128)(2,1)S(1)} %get-tuple-element.350), channel_id=1, replica_groups=mesh['graph'=16,'gr'=4,'gc'=8] {'gr','gc'}, dimensions={0}, use_global_device_ids=true | all-gather | bytes 270336 | tf_op jit(solution)/shard_map/all_gather | solution.py:81
  177.0 12.7 %all_gather.35 = bf16[128,256]{1,0:T(8,128)(2,1)S(1)} all-gather(bf16[16,256]{1,0:T(8,128)(2,1)S(1)} %get-tuple-element.349), channel_id=1, replica_groups=mesh['graph'=16,'gr'=4,'gc'=8] {'gc'}, dimensions={0}, use_global_device_ids=true | all-gather | bytes 73728 | tf_op jit(solution)/shard_map/all_gather | solution.py:77
  190.4 1.4 fusion.32
  192.4 1.1 broadcast_in_dim.67
  193.5 24.5 %while.35 = (s32[]{:T(128)}, f32[256,128]{0,1:T(8,128)S(1)}, f32[256,128]{0,1:T(8,128)S(1)}, f32[256,128]{0,1:T(8,128)S(1)}, f32[32,64,128]{2,0,1:T(8,128)}, /*i...) while((s32[]{:T(128)}, f32[256,128]{0,1:T(8,128)S(1)}, ...), condition=%wide.region_4.5_spmd.clone, body=%wide.region_0.4_spmd.clone.sunk | while | flops 107716664 | bytes 18153920 | solution.py:133
  193.5 0.7 convert_bitcast_fusion.4
  194.3 1.5 convolution_bitcast_fusion.3
  195.8 0.7 dynamic-slice_compare_fusion.2
  197.2 1.1 fusion.81
  198.3 1.2 multiply_reduce_fusion.6
  199.7 0.7 convert_bitcast_fusion.4
  200.4 1.5 convolution_bitcast_fusion.3
  201.9 0.7 dynamic-slice_compare_fusion.2
  203.3 1.1 fusion.81
  204.5 1.2 multiply_reduce_fusion.6
  205.8 0.7 convert_bitcast_fusion.4
  206.5 1.5 convolution_bitcast_fusion.3
  208.1 0.7 dynamic-slice_compare_fusion.2
  209.5 1.1 fusion.81
  210.6 1.2 multiply_reduce_fusion.6
  212.0 0.7 convert_bitcast_fusion.4
  212.7 1.5 convolution_bitcast_fusion.3
  214.2 0.7 dynamic-slice_compare_fusion.2
  215.6 1.1 fusion.81
  216.7 1.2 multiply_reduce_fusion.6
  218.1 0.7 copy.31
  218.9 0.8 copy.32
  219.8 0.8 copy.33
  220.6 1.5 fusion.31
  222.0 1.3 dynamic-slice.1
  224.2 11.9 %all-reduce.1 = bf16[128]{0:T(256)(128)(2,1)S(1)} all-reduce(bf16[128]{0:T(256)(128)(2,1)S(1)} %dynamic-update-slice.1), channel_id=1, replica_groups=mesh['graph'=16,'gr'=4,'gc'=8] {'gc'}, use_global_device_ids=true, to_apply=%add.1 | all-reduce | flops 128 | bytes 512
  236.2 1.5 multiply_reduce_fusion.2
  237.8 2.6 fusion.57
  241.0 1.0 copy.34
  242.0 1.1 all-gather.7.cloned.1.call-done
  243.1 1.2 slice.66
  244.3 29.6 %all-gather.9.cloned.1.call-done = f32[2048,128]{1,0:T(8,128)} async-done(((f32[256,128]{1,0:T(8,128)}), f32[2048,128]{1,0:T(8,128)}) %all-gather.9.cloned.1.call-update) | async-done | bytes 1048592 | tf_op jit(solution)/shard_map/all_gather | solution.py:11
  273.9 1.3 slice.67
  275.2 29.4 %all-gather.11.cloned.1.call-done = f32[2048,128]{1,0:T(8,128)} async-done(((f32[256,128]{1,0:T(8,128)}), f32[2048,128]{1,0:T(8,128)}) %all-gather.11.cloned.1.call-update) | async-done | bytes 1048592 | tf_op jit(solution)/shard_map/all_gather | solution.py:11
  304.6 1.3 slice.68
  305.9 1.6 while.34
  307.6 1.3 fusion.55
  309.1 1.5 fusion.56
  (129 shorter events, 11.0 us)
Async XLA Ops:
  7.2 80.6 %copy-start = (bf16[256,768]{1,0:T(8,128)(2,1)S(1)}, bf16[256,768]{1,0:T(8,128)(2,1)}, u32[]{:S(2)}) copy-start(bf16[256,768]{1,0:T(8,128)(2,1)} %param.32) | copy-start | bytes 1179652
  7.2 184.6 %copy-start.4 = (s32[64,128]{1,0:T(8,128)S(1)}, s32[64,128]{1,0:T(8,128)}, u32[]{:S(2)}) copy-start(s32[64,128]{1,0:T(8,128)} %param.28) | copy-start | bytes 98308
  7.2 184.6 %copy-start.7 = (f32[8,32]{1,0:T(8,128)S(1)}, f32[8,32]{1,0:T(8,128)}, u32[]{:S(2)}) copy-start(f32[8,32]{1,0:T(8,128)} %param.31) | copy-start | bytes 3076
  7.2 235.9 %all-gather.7.cloned.1.call-start = ((), (), s32[]{:S(2)}) async-start(), calls=%async_computation | async-start | bytes 1179648 | tf_op jit(solution)/shard_map/all_gather | solution.py:11
  8.5 78.3 %copy-start.15 = (bf16[16]{0:T(256)(128)(2,1)}, bf16[16]{0:T(256)(128)(2,1)S(1)}, u32[]{:S(2)}) copy-start(bf16[16]{0:T(256)(128)(2,1)S(1)} %get-tuple-element.352) | copy-start | bytes 100
  87.7 0.6 copy-start.5
  194.3 2.2 copy-start.1
  196.5 0.5 copy-start.3
  196.5 0.7 copy-start.2
  200.4 2.2 copy-start.1
  202.6 0.5 copy-start.3
  202.6 0.7 copy-start.2
  206.5 2.2 copy-start.1
  208.7 0.5 copy-start.3
  208.7 0.7 copy-start.2
  212.7 2.2 copy-start.1
  214.9 0.5 copy-start.3
  214.9 0.7 copy-start.2
  218.1 5.9 %copy-start.16 = (bf16[16]{0:T(256)(128)(2,1)S(1)}, bf16[16]{0:T(256)(128)(2,1)}, u32[]{:S(2)}) copy-start(bf16[16]{0:T(256)(128)(2,1)} %copy-done.15) | copy-start | bytes 100
  218.9 18.9 %copy-start.12 = (bf16[32,128]{1,0:T(8,128)(2,1)S(1)}, bf16[32,128]{1,0:T(8,128)(2,1)}, u32[]{:S(2)}) copy-start(bf16[32,128]{1,0:T(8,128)(2,1)} %param.38) | copy-start | bytes 24580
  218.9 18.9 %copy-start.13 = (bf16[128,32]{0,1:T(8,128)(2,1)S(1)}, bf16[128,32]{0,1:T(8,128)(2,1)}, u32[]{:S(2)}) copy-start(bf16[128,32]{0,1:T(8,128)(2,1)} %param.39) | copy-start | bytes 24580
  218.9 18.9 %copy-start.14 = (f32[32]{0:T(128)S(1)}, f32[32]{0:T(128)}, u32[]{:S(2)}) copy-start(f32[32]{0:T(128)} %param.42) | copy-start | bytes 388
  218.9 55.0 %all-gather.9.cloned.1.call-start = ((), (), s32[]{:S(2)}) async-start(), calls=%async_computation.1 | async-start | bytes 1179648 | tf_op jit(solution)/shard_map/all_gather | solution.py:11
  219.7 84.9 %all-gather.11.cloned.1.call-start = ((), (), s32[]{:S(2)}) async-start(), calls=%async_computation.2 | async-start | bytes 1179648 | tf_op jit(solution)/shard_map/all_gather | solution.py:11
  237.8 2.9 copy-start.8
  237.8 2.9 copy-start.10
  244.3 61.5 %slice-start = ((f32[2048,128]{1,0:T(8,128)}), f32[256,128]{1,0:T(8,128)S(1)}, s32[]{:S(2)}) async-start(f32[2048,128]{1,0:T(8,128)} %all-gather.7.cloned.1.call-done), calls=%async_computation.3 | async-start | bytes 262144 | tf_op jit(solution)/shard_map/slice | solution.py:12
  273.9 32.0 %slice-start.1 = ((f32[2048,128]{1,0:T(8,128)}), f32[256,128]{1,0:T(8,128)S(1)}, s32[]{:S(2)}) async-start(f32[2048,128]{1,0:T(8,128)} %all-gather.9.cloned.1.call-done), calls=%async_computation.4 | async-start | bytes 262144 | tf_op jit(solution)/shard_map/slice | solution.py:12
  304.6 1.3 slice-start.2
  305.9 1.7 copy-start.6
  305.9 4.9 %copy-start.9 = (f32[256]{0:T(256)S(1)}, f32[256]{0:T(256)}, u32[]{:S(2)}) copy-start(f32[256]{0:T(256)} %param.41) | copy-start | bytes 3076
  305.9 4.9 %copy-start.11 = (f32[16]{0:T(128)S(1)}, f32[16]{0:T(128)}, u32[]{:S(2)}) copy-start(f32[16]{0:T(128)} %get-tuple-element.351) | copy-start | bytes 196
Sparse Core Ops, SparseCore 0:
  219.0 24.0 all-gather.6
  245.2 28.6 all-gather.8
  276.1 28.4 all-gather.10
where the time goes:
time: 319 us; the launch traced here: 318 us
  blocking collectives  188 us (59%)
  waiting for transfers between devices  60.1 us (19%)
  other arithmetic  21.5 us (7%)
  matrix products  19.1 us (6%)
  between operations  15.5 us (5%)
  local copies, waits for them, and re-layouts  13.8 us (4%)
    unnamed x2, blocking collectives  88.1 us
    all_gather x3, waiting for transfers between devices, combined_all(): pieces = jax.tree.map(lambda part: lax.all_gather(part, axis), value)  60 us
    all_gather x1, blocking collectives, body(): lax.all_gather(value_own, ('gr', 'gc'), axis=0, tiled=True)  45.3 us
    all_gather x1, blocking collectives, body(): lax.all_gather(key_own, ('gr', 'gc'), axis=0, tiled=True)  41.5 us
    all_gather x1, blocking collectives, body(): lax.all_gather(query_own, 'gc', axis=0, tiled=True)  12.7 us
  transfers between devices with their start and end apart: 3, of which 3 were waited for; matrix products, arithmetic and copies ran while one was open for 4% of the time, Pallas kernels for 0%

commit v1 on v0

--- a/solution.py
+++ b/solution.py
@@ -74,7 +74,9 @@
     value_own = projected[:, 2 * width :]
     valid_own = node_mask.astype(jnp.bfloat16)
     query_rows, valid_rows = (
-        lax.all_gather(query_own, "gc", axis=0, tiled=True),
+        jnp.concatenate(
+            lax.all_to_all(jnp.stack([query_own] * lax.axis_size("gc")), "gc", 0, 0), axis=0
+        ),
         lax.all_gather(valid_own, "gc", axis=0, tiled=True),
     )
     key_all, value_all, valid_all = (

time: 319 us -> 312 us (0.978)
  blocking collectives: 188 us -> 170 us
  starting transfers between devices: 0.12 us -> 10.2 us
    all_gather x1 -> x0, blocking collectives: 12.7 us -> none  [body(): lax.all_gather(query_own, 'gc', axis=0, tiled=True)]
    all_to_all x0 -> x1, starting transfers between devices: none -> 10.1 us  [body(): lax.all_to_all(jnp.stack([query_own] * lax.axis_size('gc')), 'gc', 0, 0)]
    unnamed x2, blocking collectives: 88.1 us -> 82.8 us
  transfers between devices with their start and end apart: 3 -> 4, of which waited for: 3 -> 2; matrix products, arithmetic and copies ran while one was open for 4% -> 6% of each run, Pallas kernels for 0% -> 0%
where the time goes in v1:
time: 312 us; the launch traced here: 311 us
  blocking collectives  170 us (54%)
  waiting for transfers between devices  58.7 us (19%)
  other arithmetic  21.9 us (7%)
  matrix products  19.1 us (6%)
  between operations  15.4 us (5%)
  local copies, waits for them, and re-layouts  15.1 us (5%)
  starting transfers between devices  10.2 us (3%)
    unnamed x2, blocking collectives  82.8 us
    all_gather x3, waiting for transfers between devices, combined_all(): pieces = jax.tree.map(lambda part: lax.all_gather(part, axis), value)  58.6 us
    all_gather x1, blocking collectives, body(): lax.all_gather(value_own, ('gr', 'gc'), axis=0, tiled=True)  45.6 us
    all_gather x1, blocking collectives, body(): lax.all_gather(key_own, ('gr', 'gc'), axis=0, tiled=True)  41.5 us
    all_to_all x1, starting transfers between devices, body(): lax.all_to_all(jnp.stack([query_own] * lax.axis_size('gc')), 'gc', 0, 0)  10.1 us
  transfers between devices with their start and end apart: 4, of which 2 were waited for; matrix products, arithmetic and copies ran while one was open for 6% of the time, Pallas kernels for 0%

profile of v1, /device:TPU:1, one launch (start us, length us, event | category | flops | bytes accessed | tf_op | source)
XLA Modules:
  0.0 310.5 jit_solution(11889700111484591801)
XLA Ops:
  7.2 1.0 fusion.24
  9.4 10.1 %all-to-all-start = ((bf16[8,16,256]{2,1,0:T(8,128)(2,1)}), bf16[8,16,256]{2,1,0:T(8,128)(2,1)S(1)}, u32[]{:S(2)}, u32[]{:S(2)}) async-start(bf16[8,16,256]{2,1,0:T(8,128)(2,1)} %stack.2), calls=%async_computation | async-start | bytes 131072 | tf_op jit(solution)/shard_map/all_to_all | solution.py:78
  19.6 1.1 convert_convert_fusion
  20.7 1.3 dynamic-slice
  23.0 70.8 %all-reduce = bf16[512]{0:T(512)(128)(2,1)S(1)} all-reduce(bf16[512]{0:T(512)(128)(2,1)S(1)} %dynamic-update-slice), channel_id=1, replica_groups=mesh['graph'=16,'gr'=4,'gc'=8] {'gr','gc'}, use_global_device_ids=true, to_apply=%add | all-reduce | flops 512 | bytes 2048
  93.8 45.6 %all_gather.32 = bf16[512,256]{1,0:T(8,128)(2,1)S(1)} all-gather(bf16[16,256]{1,0:T(8,128)(2,1)S(1)} %get-tuple-element.348), channel_id=1, replica_groups=mesh['graph'=16,'gr'=4,'gc'=8] {'gr','gc'}, dimensions={0}, use_global_device_ids=true | all-gather | bytes 270336 | tf_op jit(solution)/shard_map/all_gather | solution.py:84
  139.4 41.5 %all_gather.31 = bf16[512,256]{1,0:T(8,128)(2,1)S(1)} all-gather(bf16[16,256]{1,0:T(8,128)(2,1)S(1)} %get-tuple-element.350), channel_id=1, replica_groups=mesh['graph'=16,'gr'=4,'gc'=8] {'gr','gc'}, dimensions={0}, use_global_device_ids=true | all-gather | bytes 270336 | tf_op jit(solution)/shard_map/all_gather | solution.py:83
  182.1 1.4 fusion.32
  185.4 1.1 broadcast_in_dim.67
  186.6 24.9 %while.35 = (s32[]{:T(128)}, f32[256,128]{0,1:T(8,128)S(1)}, f32[256,128]{0,1:T(8,128)S(1)}, f32[256,128]{0,1:T(8,128)S(1)}, f32[32,64,128]{2,0,1:T(8,128)}, /*i...) while((s32[]{:T(128)}, f32[256,128]{0,1:T(8,128)S(1)}, ...), condition=%wide.region_4.5_spmd.clone, body=%wide.region_0.4_spmd.clone.sunk | while | flops 107716664 | bytes 18153920 | solution.py:135
  186.6 0.7 convert_bitcast_fusion.4
  187.3 1.5 convolution_bitcast_fusion.3
  188.8 0.7 dynamic-slice_compare_fusion.2
  190.3 1.1 fusion.81
  191.4 1.2 multiply_reduce_fusion.6
  192.8 0.7 convert_bitcast_fusion.4
  193.5 1.5 convolution_bitcast_fusion.3
  195.0 0.7 dynamic-slice_compare_fusion.2
  196.5 1.1 fusion.81
  197.6 1.2 multiply_reduce_fusion.6
  199.0 0.7 convert_bitcast_fusion.4
  199.8 1.5 convolution_bitcast_fusion.3
  201.3 0.7 dynamic-slice_compare_fusion.2
  202.7 1.1 fusion.81
  203.9 1.2 multiply_reduce_fusion.6
  205.3 0.7 convert_bitcast_fusion.4
  206.0 1.5 convolution_bitcast_fusion.3
  207.5 0.7 dynamic-slice_compare_fusion.2
  209.0 1.1 fusion.81
  210.1 1.2 multiply_reduce_fusion.6
  211.5 0.7 copy.31
  212.3 0.8 copy.32
  213.2 1.3 dynamic-slice.1
  215.1 0.8 dynamic-update-slice.1
  215.9 11.9 %all-reduce.1 = bf16[128]{0:T(256)(128)(2,1)S(1)} all-reduce(bf16[128]{0:T(256)(128)(2,1)S(1)} %dynamic-update-slice.1), channel_id=1, replica_groups=mesh['graph'=16,'gr'=4,'gc'=8] {'gc'}, use_global_device_ids=true, to_apply=%add.1 | all-reduce | flops 128 | bytes 512
  227.9 0.8 copy.33
  228.6 1.5 fusion.31
  230.1 1.5 multiply_reduce_fusion.2
  231.7 2.6 fusion.57
  234.9 1.0 copy.34
  235.9 1.2 slice.66
  237.2 29.2 %all-gather.9.cloned.1.call-done = f32[2048,128]{1,0:T(8,128)} async-done(((f32[256,128]{1,0:T(8,128)}), f32[2048,128]{1,0:T(8,128)}) %all-gather.9.cloned.1.call-update) | async-done | bytes 1048592 | tf_op jit(solution)/shard_map/all_gather | solution.py:11
  266.4 1.3 slice.67
  267.7 29.4 %all-gather.11.cloned.1.call-done = f32[2048,128]{1,0:T(8,128)} async-done(((f32[256,128]{1,0:T(8,128)}), f32[2048,128]{1,0:T(8,128)}) %all-gather.11.cloned.1.call-update) | async-done | bytes 1048592 | tf_op jit(solution)/shard_map/all_gather | solution.py:11
  297.1 1.3 slice.68
  298.4 1.6 while.34
  300.1 1.3 fusion.55
  301.6 1.5 fusion.56
  (129 shorter events, 11.4 us)
Async XLA Ops:
  7.2 1.0 copy-start
  7.2 176.3 %copy-start.4 = (s32[64,128]{1,0:T(8,128)S(1)}, s32[64,128]{1,0:T(8,128)}, u32[]{:S(2)}) copy-start(s32[64,128]{1,0:T(8,128)} %param.28) | copy-start | bytes 98308
  7.2 176.3 %copy-start.7 = (f32[8,32]{1,0:T(8,128)S(1)}, f32[8,32]{1,0:T(8,128)}, u32[]{:S(2)}) copy-start(f32[8,32]{1,0:T(8,128)} %param.31) | copy-start | bytes 3076
  8.2 0.6 copy-start.5
  9.4 175.3 %all-to-all-start = ((bf16[8,16,256]{2,1,0:T(8,128)(2,1)}), bf16[8,16,256]{2,1,0:T(8,128)(2,1)S(1)}, u32[]{:S(2)}, u32[]{:S(2)}) async-start(bf16[8,16,256]{2,1,0:T(8,128)(2,1)} %stack.2), calls=%async_computation | async-start | bytes 131072 | tf_op jit(solution)/shard_map/all_to_all | solution.py:78
  19.5 216.4 %all-gather.7.cloned.1.call-start = ((), (), s32[]{:S(2)}) async-start(), calls=%async_computation.1 | async-start | bytes 1179648 | tf_op jit(solution)/shard_map/all_gather | solution.py:11
  20.7 118.7 %copy-start.15 = (bf16[16]{0:T(256)(128)(2,1)}, bf16[16]{0:T(256)(128)(2,1)S(1)}, u32[]{:S(2)}) copy-start(bf16[16]{0:T(256)(128)(2,1)S(1)} %get-tuple-element.352) | copy-start | bytes 100
  187.3 2.3 copy-start.1
  189.5 0.6 copy-start.3
  189.5 0.7 copy-start.2
  193.5 2.3 copy-start.1
  195.8 0.6 copy-start.3
  195.8 0.7 copy-start.2
  199.8 2.3 copy-start.1
  202.0 0.6 copy-start.3
  202.0 0.7 copy-start.2
  206.0 2.3 copy-start.1
  208.3 0.6 copy-start.3
  208.3 0.7 copy-start.2
  212.2 54.1 %all-gather.9.cloned.1.call-start = ((), (), s32[]{:S(2)}) async-start(), calls=%async_computation.2 | async-start | bytes 1179648 | tf_op jit(solution)/shard_map/all_gather | solution.py:11
  212.3 19.4 %copy-start.12 = (bf16[32,128]{1,0:T(8,128)(2,1)S(1)}, bf16[32,128]{1,0:T(8,128)(2,1)}, u32[]{:S(2)}) copy-start(bf16[32,128]{1,0:T(8,128)(2,1)} %param.38) | copy-start | bytes 24580
  212.3 19.4 %copy-start.13 = (bf16[128,32]{0,1:T(8,128)(2,1)S(1)}, bf16[128,32]{0,1:T(8,128)(2,1)}, u32[]{:S(2)}) copy-start(bf16[128,32]{0,1:T(8,128)(2,1)} %param.39) | copy-start | bytes 24580
  212.3 19.4 %copy-start.14 = (f32[32]{0:T(128)S(1)}, f32[32]{0:T(128)}, u32[]{:S(2)}) copy-start(f32[32]{0:T(128)} %param.42) | copy-start | bytes 388
  213.1 84.0 %all-gather.11.cloned.1.call-start = ((), (), s32[]{:S(2)}) async-start(), calls=%async_computation.3 | async-start | bytes 1179648 | tf_op jit(solution)/shard_map/all_gather | solution.py:11
  231.7 2.9 copy-start.8
  231.7 2.9 copy-start.10
  237.2 61.2 %slice-start = ((f32[2048,128]{1,0:T(8,128)}), f32[256,128]{1,0:T(8,128)S(1)}, s32[]{:S(2)}) async-start(f32[2048,128]{1,0:T(8,128)} %all-gather.7.cloned.1.call-done), calls=%async_computation.4 | async-start | bytes 262144 | tf_op jit(solution)/shard_map/slice | solution.py:12
  266.4 32.0 %slice-start.1 = ((f32[2048,128]{1,0:T(8,128)}), f32[256,128]{1,0:T(8,128)S(1)}, s32[]{:S(2)}) async-start(f32[2048,128]{1,0:T(8,128)} %all-gather.9.cloned.1.call-done), calls=%async_computation.5 | async-start | bytes 262144 | tf_op jit(solution)/shard_map/slice | solution.py:12
  297.1 1.3 slice-start.2
  298.4 1.7 copy-start.6
  298.4 4.9 %copy-start.9 = (f32[256]{0:T(256)S(1)}, f32[256]{0:T(256)}, u32[]{:S(2)}) copy-start(f32[256]{0:T(256)} %param.41) | copy-start | bytes 3076
  298.4 4.9 %copy-start.11 = (f32[16]{0:T(128)S(1)}, f32[16]{0:T(128)}, u32[]{:S(2)}) copy-start(f32[16]{0:T(128)} %get-tuple-element.351) | copy-start | bytes 196
Sparse Core Ops, SparseCore 0:
  212.4 23.3 all-gather.6
  237.9 28.4 all-gather.8
  268.6 28.4 all-gather.10
